TPU v7x, 32 devices: a whole 2x2x4 slice. The times are simulated.
32 devices in a mesh: pair: 8 (over z, y), chan: 4 (over x, core).
Axes of the slice: x: 2, y: 2, z: 4, core: 2. Of those that a mesh axis runs over, the one named last changes fastest.
Arguments:
- jones_init: float32 [512, 4, 128], P('pair', 'chan'), may hold values from -2 to 2
- dual_init: float32 [512, 4, 128], P('pair', 'chan'), may hold values from -1.2 to 1.2
- penalty: float32 [16], replicated, may hold values from 0.5 to 5
- sky_flux: float32 [4, 4, 16], P('chan'), may hold values from -0.1 to 0.5, as said below
- visibility: bfloat16 [8, 4, 8, 2, 128, 128], P('pair', 'chan'), may hold values from -4 to 4
- phases: float32 [8, 8, 2, 1024], P('pair'), may hold values from -3.1416 to 3.1416, as said below
- pair_ids: int32 [8], P('pair'), may hold values from 0 to 35, as said below
- counts: int32 [8], P('pair'), may hold values from 2 to 8, as said below
- slot_flags: int32 [8, 8], P('pair'), may hold values 0 or 1
Outputs:
- jones_final: float32 [512, 4, 128], P('pair', 'chan')
- duals_final: float32 [512, 4, 128], P('pair', 'chan')
- consensus: float32 [512, 3, 128], P('pair')
Inputs may be any that keep to these rules, and one draw needn't show every extreme that they name: `sky_flux`: [f, 0, k] and [f, 1, k] are the two polarized fluxes, [f, 2, k] and [f, 3, k] the real and imaginary cross terms. `phases`: [t, s, 0, k * 64 + p] is the phase of direction k at row station p in slot s, [t, s, 1, ...] that at column station p, before scaling by frequency. `pair_ids`: block pair of each tile, numbered row by row over blocks a <= b of 8. A tile keeps slots 0 to counts - 1; tiles whose column block lies 8 // 2 or more blocks after their row block keep all 8.
All inputs are finite; a program needn't handle non-finite values. No bound on the sum of `slot_flags` on one device may be relied on, other than what follows from the above.
Results may differ from a plain program's by a relative error of at most 0.00076.
Values sent between devices are 32-bit elements; how exact they have to be, the bound alone decides.
A program may use at most 64 MiB of HBM per device.

v0:
```python
import jax
import jax.numpy as jnp
import numpy as np
from jax import lax
from jax.sharding import PartitionSpec as P

STATIONS = 512
DIRS = 16
BLOCK = 64
TIME = 8
NPOLY = 3
ITERS = 2
STEP_SCALE = 0.3
FULL_PRECISION = lax.Precision.HIGHEST


def pair_tables(block_count):
    row_list = []
    col_list = []
    for row_block in range(block_count):
        for col_block in range(row_block, block_count):
            row_list.append(row_block)
            col_list.append(col_block)
    return (np.array(row_list, np.int32), np.array(col_list, np.int32))


def split_parts(block_jones):
    station_count = block_jones.shape[0]
    chan_count = block_jones.shape[1]
    shaped = block_jones.reshape(station_count, chan_count, 2, 2, 2, DIRS)
    shaped = jnp.transpose(shaped, (2, 1, 0, 3, 5, 4))
    return (shaped[0], shaped[1])


def sky_parts(sky_flux):
    flux_xx = sky_flux[:, 0]
    flux_yy = sky_flux[:, 1]
    cross_re = sky_flux[:, 2]
    cross_im = sky_flux[:, 3]
    zeros_k = jnp.zeros_like(flux_xx)
    real_part = jnp.stack(
        [jnp.stack([flux_xx, cross_re], -1), jnp.stack([cross_re, flux_yy], -1)], -2
    )
    imag_part = jnp.stack(
        [jnp.stack([zeros_k, cross_im], -1), jnp.stack([-cross_im, zeros_k], -1)], -2
    )
    return (real_part, imag_part)


def times_sky(parts, sky_pair):
    jones_re = parts[0][..., None]
    jones_im = parts[1][..., None]
    sky_re = sky_pair[0][:, None, None]
    sky_im = sky_pair[1][:, None, None]
    out_re = jnp.sum(jones_re * sky_re - jones_im * sky_im, axis=-2)
    out_im = jnp.sum(jones_re * sky_im + jones_im * sky_re, axis=-2)
    return (out_re, out_im)


def phase_angles(theta_side, freq_ratio):
    slot_count = theta_side.shape[0]
    shaped = jnp.transpose(theta_side.reshape(slot_count, DIRS, BLOCK), (0, 2, 1))
    angle_all = freq_ratio[:, None, None, None] * shaped[None]
    angle_all = angle_all[:, :, :, None, :, None]
    return (jnp.cos(angle_all), jnp.sin(angle_all))


def rotate_flat(parts, cosines, sines):
    part_re = parts[0][:, None]
    part_im = parts[1][:, None]
    out_re = cosines * part_re - sines * part_im
    out_im = cosines * part_im + sines * part_re
    chan_count = out_re.shape[0]
    slot_count = out_re.shape[1]
    return (
        out_re.reshape(chan_count, slot_count, 2 * BLOCK, 2 * DIRS).astype(jnp.bfloat16),
        out_im.reshape(chan_count, slot_count, 2 * BLOCK, 2 * DIRS).astype(jnp.bfloat16),
    )


def unrotate(product, cosines, sines):
    chan_count = product.shape[0]
    slot_count = product.shape[1]
    shaped = product.reshape(chan_count, slot_count, BLOCK, 2, 2, DIRS, 2)
    neg_re = shaped[:, :, :, :, 0]
    neg_im = shaped[:, :, :, :, 1]
    grad_re = -jnp.sum(neg_re * cosines + neg_im * sines, axis=1)
    grad_im = -jnp.sum(neg_im * cosines - neg_re * sines, axis=1)
    both_parts = jnp.transpose(jnp.stack([grad_re, grad_im], 0), (2, 1, 0, 3, 5, 4))
    return both_parts.reshape(BLOCK, chan_count, 8 * DIRS)


def power_rows(parts):
    power = jnp.sum(parts[0] * parts[0] + parts[1] * parts[1], axis=2)
    power = jnp.transpose(power, (1, 0, 3, 2))
    return power.reshape(power.shape[0], -1)


def slot_terms(vis_part, weights, theta_part, freq_ratio, row_sky, col_sky, col_parts, mask_wide):
    cos_row, sin_row = phase_angles(theta_part[:, 0], freq_ratio)
    cos_col, sin_col = phase_angles(theta_part[:, 1], freq_ratio)
    left_re, left_im = rotate_flat(row_sky, cos_row, sin_row)
    right_re, right_im = rotate_flat(col_sky, cos_col, sin_col)
    conj_re, conj_im = rotate_flat(col_parts, cos_col, sin_col)
    left_side = jnp.concatenate([left_re, left_im], -1)
    model_rhs = jnp.stack(
        [jnp.concatenate([conj_re, conj_im], -1), jnp.concatenate([-conj_im, conj_re], -1)], 2
    )
    predicted = jnp.einsum(
        "ftpk,ftcqk->ftcpq", left_side, model_rhs, preferred_element_type=jnp.float32
    )
    weighting = weights[None, :, None, None, None] * mask_wide
    residual = (weighting * (vis_part.astype(jnp.float32) - predicted)).astype(jnp.bfloat16)
    row_rhs = jnp.stack(
        [jnp.concatenate([right_re, right_im], -1), jnp.concatenate([-right_im, right_re], -1)], 2
    )
    col_rhs = jnp.stack(
        [jnp.concatenate([left_re, left_im], -1), jnp.concatenate([left_im, -left_re], -1)], 2
    )
    row_out = jnp.einsum("ftcpq,ftcqk->ftpk", residual, row_rhs, preferred_element_type=jnp.float32)
    col_out = jnp.einsum("ftcpq,ftcpk->ftqk", residual, col_rhs, preferred_element_type=jnp.float32)
    return (unrotate(row_out, cos_row, sin_row), unrotate(col_out, cos_col, sin_col))


def tile_terms(
    full_jones, sky_pair, freq_ratio, tables, vis_tile, theta_tile, pair_id, kept_slots, flag_row
):
    pair_range = jnp.arange(tables[0].shape[0])
    row_block = jnp.sum(jnp.where(pair_range == pair_id, tables[0], 0)).astype(jnp.int32)
    col_block = jnp.sum(jnp.where(pair_range == pair_id, tables[1], 0)).astype(jnp.int32)
    row_jones = lax.dynamic_slice_in_dim(full_jones, row_block * BLOCK, BLOCK, 0)
    col_jones = lax.dynamic_slice_in_dim(full_jones, col_block * BLOCK, BLOCK, 0)
    row_sky = times_sky(split_parts(row_jones), sky_pair)
    col_parts = split_parts(col_jones)
    col_sky = times_sky(col_parts, sky_pair)
    station_rank = jnp.arange(BLOCK)
    strict = (station_rank[:, None] < station_rank[None, :]) | (row_block != col_block)
    pair_mask = strict.astype(jnp.float32)
    mask_wide = jnp.broadcast_to(pair_mask[:, None, :, None], (BLOCK, 2, BLOCK, 2)).reshape(
        2 * BLOCK, 2 * BLOCK
    )
    weights = flag_row.astype(jnp.float32) * (jnp.arange(TIME) < kept_slots).astype(jnp.float32)
    samples = jnp.sum(weights)
    chan_count = full_jones.shape[1]
    row_grad, col_grad = slot_terms(
        vis_tile, weights, theta_tile, freq_ratio, row_sky, col_sky, col_parts, mask_wide
    )
    row_curv = samples * jnp.dot(pair_mask, power_rows(col_sky), precision=FULL_PRECISION)
    col_curv = samples * jnp.dot(pair_mask.T, power_rows(row_sky), precision=FULL_PRECISION)
    return (
        row_block,
        col_block,
        row_grad,
        col_grad,
        row_curv.reshape(BLOCK, chan_count, 2 * DIRS),
        col_curv.reshape(BLOCK, chan_count, 2 * DIRS),
    )


def add_block(total, start, piece):
    current = lax.dynamic_slice_in_dim(total, start, piece.shape[0], 0)
    return lax.dynamic_update_slice_in_dim(total, current + piece, start, 0)


def data_terms(
    full_jones, sky_pair, freq_ratio, tables, visibility, phases, pair_ids, counts, slot_flags
):
    station_count = full_jones.shape[0]
    chan_count = full_jones.shape[1]
    grad_zero = jnp.zeros((station_count, chan_count, 8 * DIRS), jnp.float32)
    curv_zero = jnp.zeros((station_count, chan_count, 2 * DIRS), jnp.float32)

    def add_tile(carry, tile_inputs):
        grad_sum, curv_sum = carry
        vis_tile, theta_tile, pair_id, kept_slots, flag_row = tile_inputs
        row_block, col_block, row_grad, col_grad, row_curv, col_curv = tile_terms(
            full_jones,
            sky_pair,
            freq_ratio,
            tables,
            vis_tile,
            theta_tile,
            pair_id,
            kept_slots,
            flag_row,
        )
        grad_sum = add_block(grad_sum, row_block * BLOCK, row_grad)
        grad_sum = add_block(grad_sum, col_block * BLOCK, col_grad)
        curv_sum = add_block(curv_sum, row_block * BLOCK, row_curv)
        curv_sum = add_block(curv_sum, col_block * BLOCK, col_curv)
        return ((grad_sum, curv_sum), None)

    totals, unused = lax.scan(
        add_tile, (grad_zero, curv_zero), (visibility, phases, pair_ids, counts, slot_flags)
    )
    return totals


def cosine_basis(chan_total):
    middle = jnp.arange(chan_total, dtype=jnp.float32) + 0.5
    degree = jnp.arange(NPOLY, dtype=jnp.float32)
    normalizer = jnp.sqrt(jnp.where(degree == 0, 1.0, 2.0) / chan_total)
    return jnp.cos(jnp.pi * middle[:, None] * degree[None, :] / chan_total) * normalizer[None, :]


def project(values_all, poly_basis):
    return jnp.sum(poly_basis[None, :, :, None] * values_all[:, :, None, :], axis=1)


def expand(coefficients, poly_basis):
    return jnp.sum(poly_basis[None, :, :, None] * coefficients[:, None, :, :], axis=2)


def jacobi(jones_now, duals_now, gradient, curvature, penalty_full, target):
    divisor = jnp.tile(curvature, (1, 1, 4)) + 0.5 * penalty_full
    return (
        jones_now
        - STEP_SCALE
        * (gradient + 0.5 * penalty_full * (jones_now - target) + 0.5 * duals_now)
        / divisor
    )


def per_device(
    jones_init, dual_init, penalty, sky_flux, visibility, phases, pair_ids, counts, slot_flags
):
    chan_dev = jones_init.shape[1]
    chan_total = chan_dev * lax.axis_size("chan")
    chan_start = lax.axis_index("chan") * chan_dev
    freq_ratio = 1.0 + (chan_start + jnp.arange(chan_dev)).astype(jnp.float32) / chan_total
    poly_basis = lax.dynamic_slice_in_dim(cosine_basis(chan_total), chan_start, chan_dev, 0)
    penalty_full = jnp.tile(penalty, 8)
    sky_pair = sky_parts(sky_flux)
    row_table, col_table = pair_tables(STATIONS // BLOCK)
    tables = (jnp.asarray(row_table), jnp.asarray(col_table))

    def every_consensus(current, dual_now):
        return lax.psum(project(current + dual_now / penalty_full, poly_basis), "chan")

    jones_now, duals_now = (
        lax.all_gather(jones_init, "pair", axis=0, tiled=True),
        lax.all_gather(dual_init, "pair", axis=0, tiled=True),
    )
    center = every_consensus(jones_now, duals_now)
    for outer_round in range(ITERS):
        target = expand(center, poly_basis)
        grad_full, curv_full = data_terms(
            jones_now,
            sky_pair,
            freq_ratio,
            tables,
            visibility,
            phases,
            pair_ids,
            counts,
            slot_flags,
        )
        gradient, curvature = lax.psum((grad_full, curv_full), "pair")
        jones_now = jacobi(jones_now, duals_now, gradient, curvature, penalty_full, target)
        center = every_consensus(jones_now, duals_now)
        duals_now = duals_now + penalty_full * (jones_now - expand(center, poly_basis))
    own_rows = jones_init.shape[0]
    own_start = lax.axis_index("pair") * own_rows
    return (
        lax.dynamic_slice_in_dim(jones_now, own_start, own_rows, 0),
        lax.dynamic_slice_in_dim(duals_now, own_start, own_rows, 0),
        lax.dynamic_slice_in_dim(center, own_start, own_rows, 0),
    )


def solution(mesh):
    in_specs = (
        P("pair", "chan", None),
        P("pair", "chan", None),
        P(),
        P("chan", None, None),
        P("pair", "chan", None, None, None, None),
        P("pair", None, None, None),
        P("pair"),
        P("pair"),
        P("pair", None),
    )
    out_specs = (P("pair", "chan", None), P("pair", "chan", None), P("pair", None, None))
    return jax.shard_map(
        per_device, mesh=mesh, in_specs=in_specs, out_specs=out_specs, check_vma=False
    )
```

profile of v0, /device:TPU:0, one launch (start us, length us, event | category | flops | bytes accessed | tf_op | source)
XLA Modules:
  0.0 485.5 jit_solution(17189194167199863357)
XLA Ops:
  11.9 32.8 %all_gather.6 = f32[512,1,128]{2,1,0:T(1,128)S(1)} all-gather(f32[64,1,128]{2,1,0:T(1,128)} %param.11), channel_id=1, replica_groups=mesh['pair'=8,'chan'=4] {'pair'}, dimensions={0}, use_global_device_ids=true | all-gather | bytes 294912 | tf_op jit(solution)/shard_map/all_gather | solution.py:241
  47.9 2.9 cosine_reduce_fusion
  61.6 2.4 mul.1652
  64.0 2.7 copy.299
  67.1 2.4 mul.1658
  69.6 2.7 copy.302
  75.6 2.5 broadcast_in_dim.77
  78.1 4.2 mul.1646
  88.8 4.4 copy.330
  93.2 7.2 %add_reduce_fusion.2 = (f32[64,2,16,2]{3,2,1,0:T(8,128)S(1)}, f32[64,2,16,2]{3,2,1,0:T(8,128)}) fusion(f32[1,8,64,2,2,16,2]{1,6,5,4,3,2,0:T(2,128)} %bitcast.414, f32[8,64,16]{0,2,1:T(8,128)S(1)} %bitcast.426, f32[8,64,16]{0,2,1:T(8,128)S(1)} %bitcast.423), kind=kLoop, calls=%fused_computation.13 | loop fusion | flops 253952 | bytes 360448 | tf_op jit(solution)/shard_map/while/body/eval_jaxpr/reduce_sum | solution.py:87
  101.4 2.4 copy.332
  106.2 2.4 copy.333
  111.3 4.4 copy.323
  115.7 7.4 %add_reduce_fusion.3 = (f32[64,2,16,2]{3,2,1,0:T(8,128)S(1)}, f32[64,2,16,2]{3,2,1,0:T(8,128)}) fusion(f32[1,8,64,2,2,16,2]{1,6,5,4,3,2,0:T(2,128)} %bitcast.415, f32[8,64,16]{0,2,1:T(8,128)S(1)} %bitcast.420, f32[8,64,16]{0,2,1:T(8,128)S(1)} %bitcast.417), kind=kLoop, calls=%fused_computation.15 | loop fusion | flops 253952 | bytes 360448 | tf_op jit(solution)/shard_map/while/body/eval_jaxpr/reduce_sum | solution.py:87
  140.2 31.0 %all_gather.7 = f32[512,1,128]{2,1,0:T(1,128)S(1)} all-gather(f32[64,1,128]{2,1,0:T(1,128)} %param.12), channel_id=1, replica_groups=mesh['pair'=8,'chan'=4] {'pair'}, dimensions={0}, use_global_device_ids=true | all-gather | bytes 294912 | tf_op jit(solution)/shard_map/all_gather | solution.py:242
  174.0 38.4 %all-reduce.18.cloned.1.call-done = (f32[512,1,128]{2,0,1:T(8,128)}, f32[512,32]{0,1:T(8,128)}) async-done(((f32[512,1,128]{2,0,1:T(8,128)}, f32[512,32]{0,1:T(8,128)}), (f32[512,1,128]{2,0,1:T(8,128)}, f32[512,32]{0,1:T(8,128)})) %all-reduce.18.cloned.1.call-update) | async-done | bytes 327696 | tf_op jit(solution)/shard_map/psum | solution.py:258
  215.8 33.2 %all-reduce.10.cloned.1.call-done = f32[512,3,128]{2,0,1:T(8,128)} async-done(((f32[512,3,128]{2,0,1:T(8,128)}), f32[512,3,128]{2,0,1:T(8,128)}) %all-reduce.10.cloned.1.call-update) | async-done | bytes 786448 | tf_op jit(solution)/shard_map/psum | solution.py:238
  296.9 4.6 copy.376
  301.6 6.2 %add_reduce_fusion = (f32[64,2,16,2]{3,2,1,0:T(8,128)S(1)}, f32[64,2,16,2]{3,2,1,0:T(8,128)S(1)}) fusion(f32[1,8,64,2,2,16,2]{1,6,5,4,3,2,0:T(2,128)} %bitcast.412, f32[8,64,16]{0,2,1:T(8,128)S(1)} %bitcast.427, f32[8,64,16]{0,2,1:T(8,128)S(1)} %bitcast.424), kind=kLoop, calls=%fused_computation.9 | loop fusion | flops 253952 | bytes 360448 | tf_op jit(solution)/shard_map/while/body/eval_jaxpr/reduce_sum | solution.py:87
  312.8 4.4 copy.368
  317.2 6.2 %add_reduce_fusion.1 = (f32[64,2,16,2]{3,2,1,0:T(8,128)S(1)}, f32[64,2,16,2]{3,2,1,0:T(8,128)S(1)}) fusion(f32[1,8,64,2,2,16,2]{1,6,5,4,3,2,0:T(2,128)} %bitcast.413, f32[8,64,16]{0,2,1:T(8,128)S(1)} %bitcast.421, f32[8,64,16]{0,2,1:T(8,128)S(1)} %bitcast.418), kind=kLoop, calls=%fused_computation.11 | loop fusion | flops 253952 | bytes 360448 | tf_op jit(solution)/shard_map/while/body/eval_jaxpr/reduce_sum | solution.py:87
  329.3 70.8 %all-reduce.16.cloned.1.call-done = (f32[512,32]{0,1:T(8,128)}, f32[512,1,128]{2,0,1:T(8,128)}) async-done(((f32[512,32]{0,1:T(8,128)}, f32[512,1,128]{2,0,1:T(8,128)}), (f32[512,32]{0,1:T(8,128)}, f32[512,1,128]{2,0,1:T(8,128)})) %all-reduce.16.cloned.1.call-update) | async-done | bytes 327696 | tf_op jit(solution)/shard_map/psum | solution.py:258
  401.0 35.5 %all-reduce.12.cloned.1.call-done = f32[512,3,128]{2,0,1:T(8,128)} async-done(((f32[512,3,128]{2,0,1:T(8,128)}), f32[512,3,128]{2,0,1:T(8,128)}) %all-reduce.12.cloned.1.call-update) | async-done | bytes 786448 | tf_op jit(solution)/shard_map/psum | solution.py:238
  440.0 35.2 %all-reduce.14.cloned.1.call-done = f32[512,3,128]{2,0,1:T(8,128)} async-done(((f32[512,3,128]{2,0,1:T(8,128)}), f32[512,3,128]{2,0,1:T(8,128)}) %all-reduce.14.cloned.1.call-update) | async-done | bytes 786448 | tf_op jit(solution)/shard_map/psum | solution.py:238
  (254 shorter events, 120.6 us)
Async XLA Ops:
  7.2 205.3 %all-reduce.18.cloned.1.call-start = ((), (), s32[]{:S(2)}) async-start(), calls=%async_computation.4 | async-start | bytes 655360 | tf_op jit(solution)/shard_map/psum | solution.py:258
  46.1 11.5 %copy-start.21 = (f32[64,2,16,2]{0,2,3,1:T(8,128)}, f32[64,2,16,2]{0,2,3,1:T(8,128)S(1)}, u32[]{:S(2)}) copy-start(f32[64,2,16,2]{0,2,3,1:T(8,128)S(1)} %get-tuple-element.97) | copy-start | bytes 49156
  46.1 12.4 %copy-start.23 = (f32[64,2,16,2]{0,2,3,1:T(8,128)}, f32[64,2,16,2]{0,2,3,1:T(8,128)S(1)}, u32[]{:S(2)}) copy-start(f32[64,2,16,2]{0,2,3,1:T(8,128)S(1)} %get-tuple-element.112) | copy-start | bytes 49156
  78.1 8.2 %copy-start.11 = (bf16[1,8,128,32]{2,3,1,0:T(8,128)(2,1)S(1)}, bf16[1,8,128,32]{2,3,1,0:T(8,128)(2,1)}, u32[]{:S(2)}) copy-start(bf16[1,8,128,32]{2,3,1,0:T(8,128)(2,1)} %get-tuple-element.141) | copy-start | bytes 196612
  78.1 8.2 %copy-start.12 = (bf16[1,8,128,32]{2,3,1,0:T(8,128)(2,1)S(1)}, bf16[1,8,128,32]{2,3,1,0:T(8,128)(2,1)}, u32[]{:S(2)}) copy-start(bf16[1,8,128,32]{2,3,1,0:T(8,128)(2,1)} %add_convert_fusion.4) | copy-start | bytes 196612
  78.1 8.2 %copy-start.30 = (bf16[1,8,128,32]{2,3,1,0:T(8,128)(2,1)S(1)}, bf16[1,8,128,32]{2,3,1,0:T(8,128)(2,1)}, u32[]{:S(2)}) copy-start(bf16[1,8,128,32]{2,3,1,0:T(8,128)(2,1)} %get-tuple-element.140) | copy-start | bytes 196612
  101.4 8.6 %copy-start.25 = (bf16[1,8,128,32]{2,3,1,0:T(8,128)(2,1)S(1)}, bf16[1,8,128,32]{2,3,1,0:T(8,128)(2,1)}, u32[]{:S(2)}) copy-start(bf16[1,8,128,32]{2,3,1,0:T(8,128)(2,1)} %get-tuple-element.142) | copy-start | bytes 196612
  101.4 8.6 %copy-start.26 = (bf16[1,8,128,32]{2,3,1,0:T(8,128)(2,1)S(1)}, bf16[1,8,128,32]{2,3,1,0:T(8,128)(2,1)}, u32[]{:S(2)}) copy-start(bf16[1,8,128,32]{2,3,1,0:T(8,128)(2,1)} %get-tuple-element.143) | copy-start | bytes 196612
  101.4 8.6 %copy-start.27 = (bf16[1,8,128,32]{2,3,1,0:T(8,128)(2,1)S(1)}, bf16[1,8,128,32]{2,3,1,0:T(8,128)(2,1)}, u32[]{:S(2)}) copy-start(bf16[1,8,128,32]{2,3,1,0:T(8,128)(2,1)} %get-tuple-element.156) | copy-start | bytes 196612
  124.2 6.6 %copy-start.35 = (f32[64,16,2]{0,1,2:T(8,128)S(1)}, f32[64,16,2]{0,1,2:T(8,128)}, u32[]{:S(2)}) copy-start(f32[64,16,2]{0,1,2:T(8,128)} %add_reduce_fusion.11) | copy-start | bytes 24580
  132.4 7.0 %copy-start.8 = (f32[512,1,128]{2,0,1:T(8,128)}, f32[512,1,128]{2,0,1:T(8,128)S(1)}, u32[]{:S(2)}) copy-start(f32[512,1,128]{2,0,1:T(8,128)S(1)} %add_dynamic-update-slice_fusion.1) | copy-start | bytes 786436
  139.4 109.6 %all-reduce.10.cloned.1.call-start = ((), (), s32[]{:S(2)}) async-start(), calls=%async_computation | async-start | bytes 1572864 | tf_op jit(solution)/shard_map/psum | solution.py:238
  140.2 110.1 %copy-start.43 = (f32[128]{0:T(128)}, f32[128]{0:T(128)S(1)}, u32[]{:S(2)}) copy-start(f32[128]{0:T(128)S(1)} %tile.32) | copy-start | bytes 1540
  172.3 80.0 %copy-start.37 = (f32[3]{0:T(128)}, f32[3]{0:T(128)S(1)}, u32[]{:S(2)}) copy-start(f32[3]{0:T(128)S(1)} %fusion.51) | copy-start | bytes 40
  173.4 226.7 %all-reduce.16.cloned.1.call-start = ((), (), s32[]{:S(2)}) async-start(), calls=%async_computation.3 | async-start | bytes 655360 | tf_op jit(solution)/shard_map/psum | solution.py:258
  214.0 44.8 %copy-start.40 = (f32[16,2,2]{0,2,1:T(2,128)S(1)}, f32[16,2,2]{0,2,1:T(2,128)}, u32[]{:S(2)}) copy-start(f32[16,2,2]{0,2,1:T(2,128)} %copy-done.39) | copy-start | bytes 772
  214.0 44.8 %copy-start.42 = (f32[16,2,2]{0,2,1:T(2,128)S(1)}, f32[16,2,2]{0,2,1:T(2,128)}, u32[]{:S(2)}) copy-start(f32[16,2,2]{0,2,1:T(2,128)} %copy-done.41) | copy-start | bytes 772
  289.0 6.4 %copy-start.13 = (bf16[1,8,128,32]{2,3,1,0:T(8,128)(2,1)S(1)}, bf16[1,8,128,32]{2,3,1,0:T(8,128)(2,1)}, u32[]{:S(2)}) copy-start(bf16[1,8,128,32]{2,3,1,0:T(8,128)(2,1)} %get-tuple-element.133) | copy-start | bytes 196612
  289.0 6.5 %copy-start.14 = (bf16[1,8,128,32]{2,3,1,0:T(8,128)(2,1)S(1)}, bf16[1,8,128,32]{2,3,1,0:T(8,128)(2,1)}, u32[]{:S(2)}) copy-start(bf16[1,8,128,32]{2,3,1,0:T(8,128)(2,1)} %add_convert_fusion.1) | copy-start | bytes 196612
  326.0 111.9 %copy-start.7 = (f32[512,1,128]{2,0,1:T(8,128)S(1)}, f32[512,1,128]{2,0,1:T(8,128)}, u32[]{:S(2)}) copy-start(f32[512,1,128]{2,0,1:T(8,128)} %copy-done.6) | copy-start | bytes 786436
  326.0 111.9 %copy-start.44 = (f32[128]{0:T(128)S(1)}, f32[128]{0:T(128)}, u32[]{:S(2)}) copy-start(f32[128]{0:T(128)} %copy-done.43) | copy-start | bytes 1540
  326.0 111.9 %copy-start.45 = (f32[128]{0:T(128)S(1)}, f32[128]{0:T(128)}, u32[]{:S(2)}) copy-start(f32[128]{0:T(128)} %broadcast_multiply_fusion.4) | copy-start | bytes 1540
  328.1 108.5 %all-reduce.12.cloned.1.call-start = ((), (), s32[]{:S(2)}) async-start(), calls=%async_computation.1 | async-start | bytes 1572864 | tf_op jit(solution)/shard_map/psum | solution.py:238
  329.2 146.0 %all-reduce.14.cloned.1.call-start = ((), (), s32[]{:S(2)}) async-start(), calls=%async_computation.2 | async-start | bytes 1572864 | tf_op jit(solution)/shard_map/psum | solution.py:238
  (27 other events, 76.5 us)
Sparse Core Ops, SparseCore 0:
  139.5 72.8 all-reduce.17
  214.8 34.1 all-reduce.9
  328.2 71.7 all-reduce.15
  402.3 34.2 all-reduce.11
  440.1 35.0 all-reduce.13
where the time goes:
time: 491 us; the launch traced here: 485 us
  waiting for transfers between devices  213 us (43%)
  local copies, waits for them, and re-layouts  108 us (22%)
  other arithmetic  72.5 us (15%)
  blocking collectives  63.7 us (13%)
  between operations  18.7 us (4%)
  matrix products  9 us (2%)
    psum x2, waiting for transfers between devices, per_device(): gradient, curvature = lax.psum((grad_full, curv_full), 'pair')  109 us
    psum x3, waiting for transfers between devices, every_consensus(): lax.psum(project(current + dual_now / penalty_full, poly_basis), 'chan')  104 us
    all_gather x1, blocking collectives, per_device(): lax.all_gather(jones_init, 'pair', axis=0, tiled=True)  32.8 us
    all_gather x1, blocking collectives, per_device(): lax.all_gather(dual_init, 'pair', axis=0, tiled=True)  31 us
    mul x20, local copies, waits for them, and re-layouts, rotate_flat(): out_re = cosines * part_re - sines * part_im  30.3 us
    reduce_sum x4, other arithmetic, unrotate(): grad_re = -jnp.sum(neg_re * cosines + neg_im * sines, axis=1)  26.9 us
  transfers between devices with their start and end apart: 5, of which 5 were waited for; matrix products, arithmetic and copies ran while one was open for 2% of the time, Pallas kernels for 0%

commit v1 on v0

--- a/solution.py
+++ b/solution.py
@@ -235,7 +235,9 @@
     tables = (jnp.asarray(row_table), jnp.asarray(col_table))
 
     def every_consensus(current, dual_now):
-        return lax.psum(project(current + dual_now / penalty_full, poly_basis), "chan")
+        return jnp.sum(
+            lax.all_gather(project(current + dual_now / penalty_full, poly_basis), "chan"), axis=0
+        )
 
     jones_now, duals_now = (
         lax.all_gather(jones_init, "pair", axis=0, tiled=True),

time: 491 us -> 419 us (0.85)
  waiting for transfers between devices: 213 us -> 136 us
    psum x3 -> x0, waiting for transfers between devices: 104 us -> none  [every_consensus(): lax.psum(project(current + dual_now / penalty_full, poly_basis), 'chan')]
    all_gather x0 -> x3, waiting for transfers between devices: none -> 27.7 us  [every_consensus(): lax.all_gather(project(current + dual_now / penalty_full, poly_basis), 'c...]
    reduce_sum x0 -> x3, other arithmetic: none -> 7.35 us  [every_consensus(): jnp.sum(lax.all_gather(project(current + dual_now / penalty_full, poly_ba...]
  transfers between devices with their start and end apart: 5 -> 5, of which waited for: 5 -> 3; matrix products, arithmetic and copies ran while one was open for 2% -> 2% of each run, Pallas kernels for 0% -> 0%
where the time goes in v1:
time: 419 us; the launch traced here: 414 us
  waiting for transfers between devices  136 us (32%)
  local copies, waits for them, and re-layouts  107 us (26%)
  other arithmetic  76.4 us (18%)
  blocking collectives  63.7 us (15%)
  between operations  20.6 us (5%)
  matrix products  9.01 us (2%)
    psum x2, waiting for transfers between devices, per_device(): gradient, curvature = lax.psum((grad_full, curv_full), 'pair')  108 us
    all_gather x1, blocking collectives, per_device(): lax.all_gather(jones_init, 'pair', axis=0, tiled=True)  32.8 us
    all_gather x1, blocking collectives, per_device(): lax.all_gather(dual_init, 'pair', axis=0, tiled=True)  31 us
    mul x20, local copies, waits for them, and re-layouts, rotate_flat(): out_re = cosines * part_re - sines * part_im  30.3 us
    all_gather x3, waiting for transfers between devices, every_consensus(): lax.all_gather(project(current + dual_now / penalty_full, poly_basis), 'c...  27.7 us
    reduce_sum x4, other arithmetic, unrotate(): grad_re = -jnp.sum(neg_re * cosines + neg_im * sines, axis=1)  26.9 us
    dot_general x2, local copies, waits for them, and re-layouts, slot_terms(): jnp.einsum('ftcpq,ftcpk->ftqk', residual, col_rhs, preferred_element_type...  9.01 us
    dot_general x2, local copies, waits for them, and re-layouts, slot_terms(): jnp.einsum('ftcpq,ftcqk->ftpk', residual, row_rhs, preferred_element_type...  8.76 us
  transfers between devices with their start and end apart: 5, of which 3 were waited for; matrix products, arithmetic and copies ran while one was open for 2% of the time, Pallas kernels for 0%

profile of v1, /device:TPU:0, one launch (start us, length us, event | category | flops | bytes accessed | tf_op | source)
XLA Modules:
  0.0 413.5 jit_solution(17554304990071902723)
XLA Ops:
  12.7 32.8 %all_gather.18 = f32[512,1,128]{2,1,0:T(1,128)S(1)} all-gather(f32[64,1,128]{2,1,0:T(1,128)} %param.11), channel_id=1, replica_groups=mesh['pair'=8,'chan'=4] {'pair'}, dimensions={0}, use_global_device_ids=true | all-gather | bytes 294912 | tf_op jit(solution)/shard_map/all_gather | solution.py:243
  48.8 2.9 cosine_reduce_fusion
  62.5 2.4 mul.1678
  64.9 2.7 copy.299
  68.0 2.4 mul.1684
  70.4 2.7 copy.302
  76.4 2.5 broadcast_in_dim.77
  79.0 4.2 %mul.1672 = f32[128,128]{1,0:T(8,128)S(1)} reshape(f32[64,2,64,2]{3,2,1,0:T(8,128)} %broadcast_in_dim.77) | data formatting | bytes 131072 | tf_op jit(solution)/shard_map/while/body/eval_jaxpr/mul | solution.py:112
  89.6 4.4 %copy.330 = f32[8,128,64]{0,2,1:T(8,128)} copy(f32[8,128,64]{1,2,0:T(8,128)S(1)} %convolution_bitcast_fusion.5) | data formatting | bytes 524288 | tf_op jit(solution)/shard_map/while/body/eval_jaxpr/ftcpq,ftcpk->ftqk/dot_general | solution.py:121
  94.0 7.2 %add_reduce_fusion.2 = (f32[64,2,16,2]{3,2,1,0:T(8,128)S(1)}, f32[64,2,16,2]{3,2,1,0:T(8,128)}) fusion(f32[1,8,64,2,2,16,2]{1,6,5,4,3,2,0:T(2,128)} %bitcast.414, f32[8,64,16]{0,2,1:T(8,128)S(1)} %bitcast.426, f32[8,64,16]{0,2,1:T(8,128)S(1)} %bitcast.423), kind=kLoop, calls=%fused_computation.13 | loop fusion | flops 253952 | bytes 360448 | tf_op jit(solution)/shard_map/while/body/eval_jaxpr/reduce_sum | solution.py:87
  102.3 2.4 copy.332
  104.7 2.3 negate_bitcast_fusion.4
  107.0 2.4 copy.333
  112.2 4.4 %copy.323 = f32[8,128,64]{0,2,1:T(8,128)} copy(f32[8,128,64]{1,2,0:T(8,128)S(1)} %convolution_bitcast_fusion.3) | data formatting | bytes 524288 | tf_op jit(solution)/shard_map/while/body/eval_jaxpr/ftcpq,ftcqk->ftpk/dot_general | solution.py:120
  116.6 7.4 %add_reduce_fusion.3 = (f32[64,2,16,2]{3,2,1,0:T(8,128)S(1)}, f32[64,2,16,2]{3,2,1,0:T(8,128)}) fusion(f32[1,8,64,2,2,16,2]{1,6,5,4,3,2,0:T(2,128)} %bitcast.415, f32[8,64,16]{0,2,1:T(8,128)S(1)} %bitcast.420, f32[8,64,16]{0,2,1:T(8,128)S(1)} %bitcast.417), kind=kLoop, calls=%fused_computation.15 | loop fusion | flops 253952 | bytes 360448 | tf_op jit(solution)/shard_map/while/body/eval_jaxpr/reduce_sum | solution.py:87
  141.1 31.0 %all_gather.19 = f32[512,1,128]{2,1,0:T(1,128)S(1)} all-gather(f32[64,1,128]{2,1,0:T(1,128)} %param.12), channel_id=1, replica_groups=mesh['pair'=8,'chan'=4] {'pair'}, dimensions={0}, use_global_device_ids=true | all-gather | bytes 294912 | tf_op jit(solution)/shard_map/all_gather | solution.py:244
  174.8 38.5 %all-reduce.9.cloned.1.call-done = (f32[512,1,128]{2,0,1:T(8,128)}, f32[512,32]{0,1:T(8,128)}) async-done(((f32[512,1,128]{2,0,1:T(8,128)}, f32[512,32]{0,1:T(8,128)}), (f32[512,1,128]{2,0,1:T(8,128)}, f32[512,32]{0,1:T(8,128)})) %all-reduce.9.cloned.1.call-update) | async-done | bytes 327696 | tf_op jit(solution)/shard_map/psum | solution.py:260
  216.7 3.0 reduce_sum.339
  267.6 4.6 %copy.376 = f32[8,128,64]{0,2,1:T(8,128)} copy(f32[8,128,64]{1,2,0:T(8,128)S(1)} %convolution_bitcast_fusion.4) | data formatting | bytes 524288 | tf_op jit(solution)/shard_map/while/body/eval_jaxpr/ftcpq,ftcpk->ftqk/dot_general | solution.py:121
  272.2 6.2 %add_reduce_fusion = (f32[64,2,16,2]{3,2,1,0:T(8,128)S(1)}, f32[64,2,16,2]{3,2,1,0:T(8,128)S(1)}) fusion(f32[1,8,64,2,2,16,2]{1,6,5,4,3,2,0:T(2,128)} %bitcast.412, f32[8,64,16]{0,2,1:T(8,128)S(1)} %bitcast.427, f32[8,64,16]{0,2,1:T(8,128)S(1)} %bitcast.424), kind=kLoop, calls=%fused_computation.9 | loop fusion | flops 253952 | bytes 360448 | tf_op jit(solution)/shard_map/while/body/eval_jaxpr/reduce_sum | solution.py:87
  283.5 4.4 %copy.368 = f32[8,128,64]{0,2,1:T(8,128)} copy(f32[8,128,64]{1,2,0:T(8,128)S(1)} %convolution_bitcast_fusion.2) | data formatting | bytes 524288 | tf_op jit(solution)/shard_map/while/body/eval_jaxpr/ftcpq,ftcqk->ftpk/dot_general | solution.py:120
  287.9 6.2 %add_reduce_fusion.1 = (f32[64,2,16,2]{3,2,1,0:T(8,128)S(1)}, f32[64,2,16,2]{3,2,1,0:T(8,128)S(1)}) fusion(f32[1,8,64,2,2,16,2]{1,6,5,4,3,2,0:T(2,128)} %bitcast.413, f32[8,64,16]{0,2,1:T(8,128)S(1)} %bitcast.421, f32[8,64,16]{0,2,1:T(8,128)S(1)} %bitcast.418), kind=kLoop, calls=%fused_computation.11 | loop fusion | flops 253952 | bytes 360448 | tf_op jit(solution)/shard_map/while/body/eval_jaxpr/reduce_sum | solution.py:87
  299.8 70.0 %all-reduce.7.cloned.1.call-done = (f32[512,32]{0,1:T(8,128)}, f32[512,1,128]{2,0,1:T(8,128)}) async-done(((f32[512,32]{0,1:T(8,128)}, f32[512,1,128]{2,0,1:T(8,128)}), (f32[512,32]{0,1:T(8,128)}, f32[512,1,128]{2,0,1:T(8,128)})) %all-reduce.7.cloned.1.call-update) | async-done | bytes 327696 | tf_op jit(solution)/shard_map/psum | solution.py:260
  374.4 27.7 %all-gather.8.cloned.1.call-done = f32[4,512,3,128]{3,1,2,0:T(8,128)} async-done(((f32[1,512,3,128]{3,1,2,0:T(8,128)}), f32[4,512,3,128]{3,1,2,0:T(8,128)}) %all-gather.8.cloned.1.call-update) | async-done | bytes 3145744 | tf_op jit(solution)/shard_map/all_gather | solution.py:239
  (259 shorter events, 118.5 us)
Async XLA Ops:
  8.0 205.3 %all-reduce.9.cloned.1.call-start = ((), (), s32[]{:S(2)}) async-start(), calls=%async_computation.4 | async-start | bytes 655360 | tf_op jit(solution)/shard_map/psum | solution.py:260
  47.0 11.5 %copy-start.21 = (f32[64,2,16,2]{0,2,3,1:T(8,128)}, f32[64,2,16,2]{0,2,3,1:T(8,128)S(1)}, u32[]{:S(2)}) copy-start(f32[64,2,16,2]{0,2,3,1:T(8,128)S(1)} %get-tuple-element.97) | copy-start | bytes 49156
  47.0 12.4 %copy-start.23 = (f32[64,2,16,2]{0,2,3,1:T(8,128)}, f32[64,2,16,2]{0,2,3,1:T(8,128)S(1)}, u32[]{:S(2)}) copy-start(f32[64,2,16,2]{0,2,3,1:T(8,128)S(1)} %get-tuple-element.112) | copy-start | bytes 49156
  70.4 6.0 %copy-start.18 = (f32[64,2,16,2]{0,2,3,1:T(8,128)S(1)}, f32[64,2,16,2]{0,2,3,1:T(8,128)}, u32[]{:S(2)}) copy-start(f32[64,2,16,2]{0,2,3,1:T(8,128)} %copy-done.17) | copy-start | bytes 49156
  70.4 6.0 %copy-start.20 = (f32[64,2,16,2]{0,2,3,1:T(8,128)S(1)}, f32[64,2,16,2]{0,2,3,1:T(8,128)}, u32[]{:S(2)}) copy-start(f32[64,2,16,2]{0,2,3,1:T(8,128)} %copy-done.19) | copy-start | bytes 49156
  73.1 5.8 %copy-start = (f32[1,8,128,32]{2,3,1,0:T(8,128)}, f32[1,8,128,32]{2,3,1,0:T(8,128)S(1)}, u32[]{:S(2)}) copy-start(f32[1,8,128,32]{2,3,1,0:T(8,128)S(1)} %copy.302) | copy-start | bytes 393220
  78.9 8.2 %copy-start.11 = (bf16[1,8,128,32]{2,3,1,0:T(8,128)(2,1)S(1)}, bf16[1,8,128,32]{2,3,1,0:T(8,128)(2,1)}, u32[]{:S(2)}) copy-start(bf16[1,8,128,32]{2,3,1,0:T(8,128)(2,1)} %get-tuple-element.141) | copy-start | bytes 196612
  78.9 8.2 %copy-start.12 = (bf16[1,8,128,32]{2,3,1,0:T(8,128)(2,1)S(1)}, bf16[1,8,128,32]{2,3,1,0:T(8,128)(2,1)}, u32[]{:S(2)}) copy-start(bf16[1,8,128,32]{2,3,1,0:T(8,128)(2,1)} %add_convert_fusion.4) | copy-start | bytes 196612
  78.9 8.2 %copy-start.30 = (bf16[1,8,128,32]{2,3,1,0:T(8,128)(2,1)S(1)}, bf16[1,8,128,32]{2,3,1,0:T(8,128)(2,1)}, u32[]{:S(2)}) copy-start(bf16[1,8,128,32]{2,3,1,0:T(8,128)(2,1)} %get-tuple-element.140) | copy-start | bytes 196612
  102.3 8.6 %copy-start.25 = (bf16[1,8,128,32]{2,3,1,0:T(8,128)(2,1)S(1)}, bf16[1,8,128,32]{2,3,1,0:T(8,128)(2,1)}, u32[]{:S(2)}) copy-start(bf16[1,8,128,32]{2,3,1,0:T(8,128)(2,1)} %get-tuple-element.142) | copy-start | bytes 196612
  102.3 8.6 %copy-start.26 = (bf16[1,8,128,32]{2,3,1,0:T(8,128)(2,1)S(1)}, bf16[1,8,128,32]{2,3,1,0:T(8,128)(2,1)}, u32[]{:S(2)}) copy-start(bf16[1,8,128,32]{2,3,1,0:T(8,128)(2,1)} %get-tuple-element.143) | copy-start | bytes 196612
  102.3 8.6 %copy-start.27 = (bf16[1,8,128,32]{2,3,1,0:T(8,128)(2,1)S(1)}, bf16[1,8,128,32]{2,3,1,0:T(8,128)(2,1)}, u32[]{:S(2)}) copy-start(bf16[1,8,128,32]{2,3,1,0:T(8,128)(2,1)} %get-tuple-element.156) | copy-start | bytes 196612
  125.0 6.6 %copy-start.36 = (f32[64,16,2]{0,1,2:T(8,128)S(1)}, f32[64,16,2]{0,1,2:T(8,128)}, u32[]{:S(2)}) copy-start(f32[64,16,2]{0,1,2:T(8,128)} %add_reduce_fusion.11) | copy-start | bytes 24580
  133.2 7.0 %copy-start.8 = (f32[512,1,128]{2,0,1:T(8,128)}, f32[512,1,128]{2,0,1:T(8,128)S(1)}, u32[]{:S(2)}) copy-start(f32[512,1,128]{2,0,1:T(8,128)S(1)} %add_dynamic-update-slice_fusion.1) | copy-start | bytes 786436
  140.3 76.4 %all-gather.4.cloned.1.call-start = ((), (), s32[]{:S(2)}) async-start(), calls=%async_computation | async-start | bytes 3932160 | tf_op jit(solution)/shard_map/all_gather | solution.py:239
  141.1 79.9 %copy-start.44 = (f32[128]{0:T(128)}, f32[128]{0:T(128)S(1)}, u32[]{:S(2)}) copy-start(f32[128]{0:T(128)S(1)} %tile.32) | copy-start | bytes 1540
  173.1 46.5 %copy-start.38 = (f32[3]{0:T(128)}, f32[3]{0:T(128)S(1)}, u32[]{:S(2)}) copy-start(f32[3]{0:T(128)S(1)} %fusion.51) | copy-start | bytes 40
  174.2 195.6 %all-reduce.7.cloned.1.call-start = ((), (), s32[]{:S(2)}) async-start(), calls=%async_computation.3 | async-start | bytes 655360 | tf_op jit(solution)/shard_map/psum | solution.py:260
  219.7 9.7 %copy-start.41 = (f32[16,2,2]{0,2,1:T(2,128)S(1)}, f32[16,2,2]{0,2,1:T(2,128)}, u32[]{:S(2)}) copy-start(f32[16,2,2]{0,2,1:T(2,128)} %copy-done.40) | copy-start | bytes 772
  219.7 9.7 %copy-start.43 = (f32[16,2,2]{0,2,1:T(2,128)S(1)}, f32[16,2,2]{0,2,1:T(2,128)}, u32[]{:S(2)}) copy-start(f32[16,2,2]{0,2,1:T(2,128)} %copy-done.42) | copy-start | bytes 772
  259.7 6.4 %copy-start.13 = (bf16[1,8,128,32]{2,3,1,0:T(8,128)(2,1)S(1)}, bf16[1,8,128,32]{2,3,1,0:T(8,128)(2,1)}, u32[]{:S(2)}) copy-start(bf16[1,8,128,32]{2,3,1,0:T(8,128)(2,1)} %get-tuple-element.133) | copy-start | bytes 196612
  259.7 6.5 %copy-start.14 = (bf16[1,8,128,32]{2,3,1,0:T(8,128)(2,1)S(1)}, bf16[1,8,128,32]{2,3,1,0:T(8,128)(2,1)}, u32[]{:S(2)}) copy-start(bf16[1,8,128,32]{2,3,1,0:T(8,128)(2,1)} %add_convert_fusion.1) | copy-start | bytes 196612
  298.7 72.2 %all-gather.6.cloned.1.call-start = ((), (), s32[]{:S(2)}) async-start(), calls=%async_computation.1 | async-start | bytes 3932160 | tf_op jit(solution)/shard_map/all_gather | solution.py:239
  299.8 102.3 %all-gather.8.cloned.1.call-start = ((), (), s32[]{:S(2)}) async-start(), calls=%async_computation.2 | async-start | bytes 3932160 | tf_op jit(solution)/shard_map/all_gather | solution.py:239
  (28 other events, 68.2 us)
Sparse Core Ops, SparseCore 0:
  140.4 72.8 all-reduce.8
  298.8 70.9 all-reduce.6
Sparse Core Ops, SparseCore 1:
  174.3 29.9 all-gather.3
  300.7 27.6 all-gather.5
  374.5 27.6 all-gather.7
